TPU v7x, 32 devices: a whole 2x2x4 slice. The times are simulated.
32 devices in a mesh: grp: 2 (over x), tile: 16 (over z, y, core).
Axes of the slice: x: 2, y: 2, z: 4, core: 2. Of those that a mesh axis runs over, the one named last changes fastest.
Arguments:
- visibility: bfloat16 [32, 16, 2, 256, 256], P('tile', 'grp'), parts along dimension 1, may hold values from -12 to 12
- station_beam: bfloat16 [16, 2, 512, 2048], P('grp', None, 'tile'), parts along dimension 0, may hold values from -4.1875 to 4.1875
- antenna_uvw: float32 [16, 3, 2048], P('grp'), parts along dimension 0, may hold values from -40 to 40
- source_dirs: float32 [2, 4096], P(None, 'tile'), may hold values from -0.4 to 0.4
- source_flux: bfloat16 [8192], P(('grp', 'tile')), parts along dimension 0, may hold values from 0.0029907227 to 0.029907227
- visible_list: int32 [8, 512], P(None, 'tile'), may hold values from 0 to 255
- antenna_flags: int32 [16, 2048], P('grp'), parts along dimension 0, may hold values 0 or 1
Outputs:
- residual: bfloat16 [32, 16, 2, 256, 256], P('tile', 'grp'), parts along dimension 1
- flux_grad: float32 [16, 512], P('grp', 'tile'), parts along dimension 0
There are 2 independent parts, one for each index of `grp`. A program takes and returns all parts, laid end to end along the dimension named above; an argument that names none is the same for every part. Nothing has to cross between parts.
Inputs may be any that keep to these rules, and one draw needn't show every extreme that they name: `visible_list`: entry k of a slot names pool source 256 * (k // 32) + value, a source of its own group. `antenna_flags`: 1 marks a flagged antenna.
All inputs are finite; a program needn't handle non-finite values.
Results may differ from a plain program's by a relative error of at most 0.0034.
Values may be sent and summed in bfloat16 or wider, within the bound.
A program may use at most 192 MiB of HBM per device.

v0:
```python
import math
import jax
import jax.numpy as jnp
import numpy as np
from jax import lax
from jax.sharding import PartitionSpec as P

BLOCKS = 8
two_pi = 2.0 * math.pi


def unit_table(block_count):
    first_list = []
    second_list = []
    diag_list = []
    for row_block in range(block_count):
        for col_block in range(row_block + 1, block_count):
            first_list.append(row_block)
            second_list.append(col_block)
            diag_list.append(0)
    for pair_index in range(block_count // 2):
        first_list.append(2 * pair_index)
        second_list.append(2 * pair_index + 1)
        diag_list.append(1)
    return (
        np.array(first_list, np.int32),
        np.array(second_list, np.int32),
        np.array(diag_list, np.int32),
    )


def build_factors(station_beam, antenna_uvw, source_dirs, source_flux, visible_list):
    pool_size = source_dirs.shape[1]
    chosen = visible_list[:, :, None] == jnp.arange(pool_size, dtype=jnp.int32)[None, None, :]
    coord_east = jnp.sum(jnp.where(chosen, source_dirs[0][None, None, :], 0.0), axis=2)
    coord_north = jnp.sum(jnp.where(chosen, source_dirs[1][None, None, :], 0.0), axis=2)
    brightness = jnp.sum(
        jnp.where(chosen, source_flux.astype(jnp.float32)[None, None, :], 0.0), axis=2
    ).astype(jnp.bfloat16)
    depth_term = jnp.sqrt(1.0 - coord_east * coord_east - coord_north * coord_north) - 1.0
    delay_sum = (
        antenna_uvw[:, 0, None, :] * coord_east[:, :, None]
        + antenna_uvw[:, 1, None, :] * coord_north[:, :, None]
        + antenna_uvw[:, 2, None, :] * depth_term[:, :, None]
    )
    phases = two_pi * delay_sum
    cosine = jnp.cos(phases)
    sine = jnp.sin(phases)
    beam_f = station_beam.astype(jnp.float32)
    real_part = beam_f[:, 0] * cosine + beam_f[:, 1] * sine
    imag_part = beam_f[:, 1] * cosine - beam_f[:, 0] * sine
    return (jnp.stack([real_part, imag_part], 1).astype(jnp.bfloat16), brightness)


def predict(rows_f, cols_f, brightness):
    scaled = (rows_f.astype(jnp.float32) * brightness.astype(jnp.float32)[:, None, :, None]).astype(
        jnp.bfloat16
    )
    turned = jnp.stack([scaled[:, 1], -scaled[:, 0]], 1)
    stacked = jnp.stack([scaled, turned], 1)
    return jnp.einsum("tdckr,tckq->tdrq", stacked, cols_f, preferred_element_type=jnp.float32)


def pull_back(resid, rows_f, cols_f):
    rstack = jnp.stack(
        [jnp.stack([resid[:, 0], -resid[:, 1]], 1), jnp.stack([resid[:, 1], resid[:, 0]], 1)], 1
    )
    pulled = jnp.einsum("tdcrq,tckq->tdkr", rstack, cols_f, preferred_element_type=jnp.float32)
    return jnp.sum(rows_f.astype(jnp.float32) * pulled, axis=(1, 3))


def unit_work(block_one, block_two, diag_tile, bright_all, vis_unit, keep_one, keep_two):
    span = vis_unit.shape[3]
    local_ids = jnp.arange(span, dtype=jnp.int32)
    upper_part = local_ids[:, None] < local_ids[None, :]
    lower_part = local_ids[:, None] > local_ids[None, :]
    cols_one = jnp.where(diag_tile, block_one, block_two)
    first_pred = predict(block_one, cols_one, bright_all)
    pred_shape = first_pred.shape
    second_pred = lax.cond(
        diag_tile,
        lambda: predict(block_two, block_two, bright_all),
        lambda: jnp.zeros(pred_shape, jnp.float32),
    )
    first_mask = jnp.logical_or(jnp.logical_not(diag_tile), upper_part)
    predicted = jnp.where(first_mask[None, None], first_pred, jnp.swapaxes(second_pred, 2, 3))
    upper_f = upper_part.astype(jnp.float32)
    lower_f = lower_part.astype(jnp.float32)
    off_weight = keep_one[:, :, None] * keep_two[:, None, :]
    diag_weight = (
        upper_f[None] * keep_one[:, :, None] * keep_one[:, None, :]
        + lower_f[None] * keep_two[:, :, None] * keep_two[:, None, :]
    )
    weights = jnp.where(diag_tile, diag_weight, off_weight)
    residual = (weights[:, None] * (vis_unit.astype(jnp.float32) - predicted)).astype(jnp.bfloat16)
    zero_res = jnp.zeros_like(residual)
    first_res = jnp.where(first_mask[None, None], residual, zero_res)
    partial_value = pull_back(first_res, block_one, cols_one)
    second_sel = jnp.logical_and(diag_tile, lower_part)
    grad_shape = partial_value.shape
    second_part = lax.cond(
        diag_tile,
        lambda: pull_back(
            jnp.swapaxes(jnp.where(second_sel[None, None], residual, zero_res), 2, 3),
            block_two,
            block_two,
        ),
        lambda: jnp.zeros(grad_shape, jnp.float32),
    )
    return (residual, partial_value + second_part)


def per_device(
    visibility, station_beam, antenna_uvw, source_dirs, source_flux, visible_list, antenna_flags
):
    tile_count = lax.axis_size("tile")
    units_dev = visibility.shape[0]
    span = visibility.shape[4]
    slot_count = station_beam.shape[0]
    per_group = station_beam.shape[2]
    antennas = station_beam.shape[3]
    tile_index = lax.axis_index("tile")
    first_tab, second_tab, diag_tab = unit_table(BLOCKS)
    first_arr = jnp.asarray(first_tab)
    second_arr = jnp.asarray(second_tab)
    diag_arr = jnp.asarray(diag_tab)
    keep_all = 1.0 - antenna_flags.astype(jnp.float32)
    owned, brightness = build_factors(
        station_beam, antenna_uvw, source_dirs, source_flux, visible_list
    )
    gathered, bright_all = (
        lax.all_gather(owned, "tile", axis=2, tiled=True),
        lax.all_gather(brightness, "tile", axis=1, tiled=True),
    )
    residuals = []
    partial_total = jnp.zeros((slot_count, per_group * tile_count), jnp.float32)
    for unit_slot in range(units_dev):
        unit_id = tile_index * units_dev + unit_slot
        start_one = (first_arr[unit_id] * span).astype(jnp.int32)
        start_two = (second_arr[unit_id] * span).astype(jnp.int32)
        diag_tile = diag_arr[unit_id] == 1
        block_one = lax.dynamic_slice_in_dim(gathered, start_one, span, 3)
        block_two = lax.dynamic_slice_in_dim(gathered, start_two, span, 3)
        keep_one = lax.dynamic_slice_in_dim(keep_all, start_one, span, 1)
        keep_two = lax.dynamic_slice_in_dim(keep_all, start_two, span, 1)
        residual, partial_value = unit_work(
            block_one, block_two, diag_tile, bright_all, visibility[unit_slot], keep_one, keep_two
        )
        residuals.append(residual)
        partial_total = partial_total + partial_value
    summed = lax.psum_scatter(partial_total, "tile", scatter_dimension=1, tiled=True)
    flux_grad = summed * (-1.0 / (8.0 * antennas))
    return (jnp.stack(residuals, 0), flux_grad)


def solution(mesh):
    return jax.shard_map(
        per_device,
        mesh=mesh,
        in_specs=(
            P("tile", "grp", None, None, None),
            P("grp", None, "tile", None),
            P("grp", None, None),
            P(None, "tile"),
            P(("grp", "tile")),
            P(None, "tile"),
            P("grp", None),
        ),
        out_specs=(P("tile", "grp", None, None, None), P("grp", "tile")),
        check_vma=False,
    )
```

profile of v0, /device:TPU:0, one launch (start us, length us, event | category | flops | bytes accessed | tf_op | source)
XLA Modules:
  0.0 425.8 jit_solution(3471020011920112316)
XLA Ops:
  7.2 0.8 fusion.93
  8.0 0.7 convert_element_type.108
  8.6 0.9 slice_bitcast_fusion.2
  9.6 2.1 convert_element_type.106
  11.7 0.3 select_reduce_fusion
  12.0 8.9 %add_convert_fusion = (bf16[8,1,32,2048]{3,2,1,0:T(8,128)(2,1)S(1)}, bf16[8,1,32,2048]{3,2,1,0:T(8,128)(2,1)S(1)}) fusion(f32[8,2,32,2048]{3,2,1,0:T(8,128)S(1)} %convert_element_type.106, f32[8,32]{1,0:T(8,128)S(1)} %sqrt_add_fusion, f32[8,2048]{1,0:T(8,128)S(1)} %get-tuple-element.134, f32[8,32]{1,0:T(8,128)S(1)} %get-tuple-element.95, ...), kind=kLoop, calls=%fused_computation.93 | loop fusion | flops 7340032 | bytes 6491136 | tf_op jit(solution)/shard_map/convert.2
  20.9 0.2 pad_maximum_fusion.4
  21.2 2.5 copy.115
  23.8 0.7 fusion.94
  27.0 0.7 fusion.96
  29.1 23.9 %all-gather = bf16[16,32,8]{1,2,0:T(8,128)(2,1)S(1)} all-gather(bf16[1,32,8]{1,2,0:T(8,128)(2,1)S(1)} %bitcast.185), channel_id=1, replica_groups=mesh['grp'=2,'tile'=16] {'tile'}, dimensions={0}, use_global_device_ids=true | all-gather | bytes 8704 | tf_op jit(solution)/shard_map/all_gather | solution.py:133
  53.4 2.7 multiply_select_fusion.1
  56.1 138.6 %all-gather.3.cloned.1.call-done = bf16[8,2,512,2048]{3,0,1,2:T(8,128)(2,1)} async-done(((bf16[8,2,32,2048]{3,0,1,2:T(8,128)(2,1)}), bf16[8,2,512,2048]{3,0,1,2:T(8,128)(2,1)}) %all-gather.3.cloned.1.call-update) | async-done | bytes 33554448 | tf_op jit(solution)/shard_map/all_gather | solution.py:132
  194.7 12.4 %constant_dynamic-slice_fusion.5 = (bf16[8,2,512,256]{3,0,1,2:T(8,128)(2,1)}, bf16[8,2,512,256]{3,0,1,2:T(8,128)(2,1)}, bf16[8,2,512,256]{3,0,1,2:T(8,128)(2,1)}, bf16[8,2,512,256]{3,0,1,2:T(8,128)(2,1)}) fusion(bf16[8,2,512,2048]{3,0,1,2:T(8,128)(2,1)} %all-gather.3.cloned.1.call-done, s32[]{:T(128)S(6)} %select_n.94, s32[]{:T(128)S(6)} %select_n.105, ...), kind=kLoop, calls=%fused_computation.123 | loop fusion | bytes 33554448 | tf_op jit(solution)/shard_map/dynamic_slice | solution.py:142
  207.1 7.6 %copy.167 = bf16[8,2,512,256]{2,3,1,0:T(8,128)(2,1)} copy(bf16[8,2,512,256]{3,0,1,2:T(8,128)(2,1)} %get-tuple-element.111) | data formatting | bytes 8388608
  214.7 7.6 %copy.169 = bf16[8,2,512,256]{2,3,1,0:T(8,128)(2,1)} copy(bf16[8,2,512,256]{3,0,1,2:T(8,128)(2,1)} %get-tuple-element.112) | data formatting | bytes 8388608
  222.3 7.5 %fusion.44 = (bf16[8,2,512,256]{2,3,1,0:T(8,128)(2,1)S(1)}, bf16[8,2,512,256]{2,3,1,0:T(8,128)(2,1)}) fusion(bf16[8,2,512,256]{2,3,1,0:T(8,128)(2,1)} %copy.167, f32[8,512]{1,0:T(8,128)S(1)} %bitcast_convert_fusion, bf16[8,2,512,256]{2,3,1,0:T(8,128)(2,1)} %copy.169), kind=kLoop, calls=%fused_computation.50 | loop fusion | flops 12582912 | bytes 16793600 | tf_op jit(solution)/shard_map/convert_element_type | solution.py:56
  229.8 1.9 fusion.91
  231.7 0.8 copy-done.9
  232.4 7.6 %copy.168 = bf16[8,2,512,256]{2,3,1,0:T(8,128)(2,1)} copy(bf16[8,2,512,256]{3,0,1,2:T(8,128)(2,1)} %get-tuple-element.113) | data formatting | bytes 8388608
  240.1 2.5 conditional.4
  240.1 2.5 broadcast.220
  242.5 5.4 %copy.121 = f32[8,2,256,256]{2,3,1,0:T(8,128)} copy(f32[8,2,256,256]{3,2,1,0:T(8,128)} %get-tuple-element.156) | data formatting | bytes 8388608 | tf_op jit(solution)/shard_map/cond | solution.py:80
  248.0 4.3 %maximum_bitcast_fusion.6 = bf16[8,1,2,512,256]{3,4,2,1,0:T(8,128)(2,1)} fusion(bf16[8,1,512,256]{2,3,1,0:T(8,128)(2,1)} %get-tuple-element.118, bf16[8,1,512,256]{2,3,1,0:T(8,128)(2,1)S(1)} %get-tuple-element.117), kind=kLoop, calls=%fused_computation.61 | loop fusion | flops 2097152 | bytes 8388608 | tf_op jit(solution)/shard_map/stack | solution.py:60
  252.3 1.3 copy-done.6
  253.6 8.4 %broadcast_select_fusion.3 = (bf16[8,2,256,256]{3,2,1,0:T(8,128)(2,1)S(1)}, bf16[8,2,256,256]{3,2,1,0:T(8,128)(2,1)}) fusion(pred[256,256]{1,0:T(8,128)(4,1)S(1)} %fusion.85, f32[8,2,256,256]{2,3,1,0:T(8,128)} %copy.121, bf16[8,2,512,256]{2,3,1,0:T(8,128)(2,1)S(1)} %copy-done.6, bf16[8,2,512,256]{2,3,1,0:T(8,128)(2,1)S(1)} %copy-done, pred[]{:T(512)} %bitcast.28, ...), kind=kOutput, calls=%fused_computation.99 | convolution fusion | flops 2160066560 | bytes 29425664 | tf_op jit(solution)/shard_map/tdckr,tckq->tdrq/dot_general | solution.py:61
  262.0 1.8 slice_negate_fusion.7
  263.8 1.6 copy-done.7
  265.3 1.6 fusion.92
  266.9 7.5 %copy.170 = bf16[8,2,512,256]{2,3,1,0:T(8,128)(2,1)} copy(bf16[8,2,512,256]{3,0,1,2:T(8,128)(2,1)} %get-tuple-element.114) | data formatting | bytes 8388608
  274.4 2.5 conditional.5
  274.4 2.5 broadcast.221
  276.9 5.3 %copy.126 = f32[8,2,256,256]{2,3,1,0:T(8,128)} copy(f32[8,2,256,256]{3,2,1,0:T(8,128)} %get-tuple-element.157) | data formatting | bytes 8388608 | tf_op jit(solution)/shard_map/cond | solution.py:80
  282.2 4.3 %maximum_bitcast_fusion.7 = bf16[8,1,2,512,256]{3,4,2,0,1:T(8,128)(2,1)} fusion(bf16[8,1,512,256]{2,3,1,0:T(8,128)(2,1)} %get-tuple-element.120, bf16[8,1,512,256]{2,3,1,0:T(8,128)(2,1)S(1)} %get-tuple-element.119), kind=kLoop, calls=%fused_computation.62 | loop fusion | flops 2097152 | bytes 8388608 | tf_op jit(solution)/shard_map/stack | solution.py:60
  286.5 1.3 copy-done.8
  287.8 8.8 %broadcast_select_fusion.2 = (bf16[8,2,256,256]{3,2,1,0:T(8,128)(2,1)S(1)}, bf16[8,2,256,256]{3,2,1,0:T(8,128)(2,1)}) fusion(pred[256,256]{1,0:T(8,128)(4,1)S(1)} %fusion.84, f32[8,2,256,256]{2,3,1,0:T(8,128)} %copy.126, bf16[8,2,512,256]{2,3,1,0:T(8,128)(2,1)S(1)} %copy-done.4, bf16[8,2,512,256]{2,3,1,0:T(8,128)(2,1)} %copy.170, pred[]{:T(512)} %bitcast.48, ...), kind=kOutput, calls=%fused_computation.98 | convolution fusion | flops 2160066560 | bytes 29425664 | tf_op jit(solution)/shard_map/tdckr,tckq->tdrq/dot_general | solution.py:61
  296.6 1.8 slice_negate_fusion.6
  298.4 1.2 copy-done.10
  299.6 4.5 %maximum_bitcast_fusion.8 = (bf16[8,1,2,256,256]{4,3,2,0,1:T(8,128)(2,1)}, bf16[8,1,2,256,256]{4,3,2,0,1:T(8,128)(2,1)}) fusion(bf16[8,1,256,256]{3,2,1,0:T(8,128)(2,1)S(1)} %copy-done.10, bf16[8,1,256,256]{3,2,1,0:T(8,128)(2,1)} %get-tuple-element.123, bf16[8,1,256,256]{3,2,1,0:T(8,128)(2,1)} %get-tuple-element.122), kind=kLoop, calls=%fused_computation.87 | loop fusion | flops 2097152 | bytes 7340032 | tf_op jit(solution)/shard_map/stack | solution.py:65
  304.2 6.4 %fusion.45 = f32[8,512]{1,0:T(8,128)S(1)} fusion(bf16[8,2,512,256]{2,3,1,0:T(8,128)(2,1)} %copy.167, bf16[8,2,512,256]{2,3,1,0:T(8,128)(2,1)S(1)} %copy-done.1, pred[]{:T(512)} %bitcast.28, bf16[8,1,2,256,256]{4,3,2,0,1:T(8,128)(2,1)} %get-tuple-element.128, bf16[8,1,2,256,256]{4,3,2,0,1:T(8,128)(2,1)} %get-tuple-element.127), kind=kOutput, calls=%fused_computation.51 | convolution fusion | flops 2157965312 | bytes 12599297 | tf_op jit(solution)/shard_map/tdcrq,tckq->tdkr/dot_general | solution.py:68
  310.7 4.1 maximum_bitcast_fusion.10
  314.8 6.4 %fusion.47 = f32[8,512]{1,0:T(8,128)S(1)} fusion(bf16[8,2,512,256]{2,3,1,0:T(8,128)(2,1)S(1)} %copy-done.5, bf16[8,2,512,256]{2,3,1,0:T(8,128)(2,1)} %copy.170, pred[]{:T(512)} %bitcast.48, bf16[8,1,2,256,256]{4,3,2,0,1:T(8,128)(2,1)} %get-tuple-element.130, bf16[8,1,2,256,256]{4,3,2,0,1:T(8,128)(2,1)} %get-tuple-element.129), kind=kOutput, calls=%fused_computation.53 | convolution fusion | flops 2157965312 | bytes 12599297 | tf_op jit(solution)/shard_map/tdcrq,tckq->tdkr/dot_general | solution.py:68
  321.2 0.3 conditional.7
  321.5 0.9 copy.165
  322.4 4.6 %pad_maximum_fusion.1 = bf16[2,8,2,256,256]{4,3,2,1,0:T(8,128)(2,1)} fusion(bf16[1,8,2,256,256]{4,3,2,1,0:T(8,128)(2,1)} %bitcast.180, bf16[1,8,2,256,256]{4,3,2,1,0:T(8,128)(2,1)} %bitcast.179), kind=kLoop, calls=%fused_computation.63 | loop fusion | flops 2097152 | bytes 8388608 | tf_op jit(solution)/shard_map/stack | solution.py:153
  327.0 90.5 %reduce-scatter.4.cloned.1.call-done = f32[32,8]{1,0:T(8,128)} async-done(((f32[512,8]{1,0:T(8,128)}), f32[32,8]{1,0:T(8,128)}) %reduce-scatter.4.cloned.1.call-update) | async-done | bytes 1040
  417.5 0.8 copy.166
  418.3 0.6 broadcast_multiply_fusion
  (47 shorter events, 0.6 us)
Async XLA Ops:
  7.2 4.5 %copy-start.15 = (s32[8,32]{1,0:T(8,128)S(1)}, s32[8,32]{1,0:T(8,128)}, u32[]{:S(2)}) copy-start(s32[8,32]{1,0:T(8,128)} %param.23) | copy-start | bytes 3076
  7.2 187.5 %all-gather.3.cloned.1.call-start = ((), (), s32[]{:S(2)}) async-start(), calls=%async_computation.1 | async-start | bytes 35651584 | tf_op jit(solution)/shard_map/all_gather | solution.py:132
  21.1 2.6 copy-start.17
  21.2 2.6 copy-start.18
  21.2 5.9 %copy-start.16 = (s32[32]{0:T(128)S(1)}, s32[32]{0:T(128)}, u32[]{:S(2)}) copy-start(s32[32]{0:T(128)} %constant.62.clone) | copy-start | bytes 388
  21.2 32.1 %copy-start.14 = (s32[8,2048]{1,0:T(8,128)S(1)}, s32[8,2048]{1,0:T(8,128)}, u32[]{:S(2)}) copy-start(s32[8,2048]{1,0:T(8,128)} %param.24) | copy-start | bytes 196612
  23.7 393.8 %reduce-scatter.4.cloned.1.call-start = ((), (), s32[]{:S(2)}) async-start(), calls=%async_computation.2 | async-start | bytes 278528
  229.8 2.7 copy-start.9
  248.0 4.3 %copy-start = (bf16[8,2,512,256]{2,3,1,0:T(8,128)(2,1)S(1)}, bf16[8,2,512,256]{2,3,1,0:T(8,128)(2,1)}, u32[]{:S(2)}) copy-start(bf16[8,2,512,256]{2,3,1,0:T(8,128)(2,1)} %copy.168) | copy-start | bytes 12582916
  248.0 5.6 %copy-start.6 = (bf16[8,2,512,256]{2,3,1,0:T(8,128)(2,1)S(1)}, bf16[8,2,512,256]{2,3,1,0:T(8,128)(2,1)}, u32[]{:S(2)}) copy-start(bf16[8,2,512,256]{2,3,1,0:T(8,128)(2,1)} %copy.167) | copy-start | bytes 12582916
  262.0 3.3 copy-start.7
  282.2 4.3 %copy-start.4 = (bf16[8,2,512,256]{2,3,1,0:T(8,128)(2,1)S(1)}, bf16[8,2,512,256]{2,3,1,0:T(8,128)(2,1)}, u32[]{:S(2)}) copy-start(bf16[8,2,512,256]{2,3,1,0:T(8,128)(2,1)} %copy.169) | copy-start | bytes 12582916
  282.2 5.6 %copy-start.8 = (bf16[8,2,512,256]{2,3,1,0:T(8,128)(2,1)S(1)}, bf16[8,2,512,256]{2,3,1,0:T(8,128)(2,1)}, u32[]{:S(2)}) copy-start(bf16[8,2,512,256]{2,3,1,0:T(8,128)(2,1)} %get-tuple-element.141) | copy-start | bytes 12582916
  298.4 1.2 copy-start.10
  298.4 5.8 %copy-start.1 = (bf16[8,2,512,256]{2,3,1,0:T(8,128)(2,1)S(1)}, bf16[8,2,512,256]{2,3,1,0:T(8,128)(2,1)}, u32[]{:S(2)}) copy-start(bf16[8,2,512,256]{2,3,1,0:T(8,128)(2,1)} %copy.168) | copy-start | bytes 12582916
  304.2 6.5 %copy-start.11 = (bf16[8,1,256,256]{3,2,1,0:T(8,128)(2,1)S(1)}, bf16[8,1,256,256]{3,2,1,0:T(8,128)(2,1)}, u32[]{:S(2)}) copy-start(bf16[8,1,256,256]{3,2,1,0:T(8,128)(2,1)} %get-tuple-element.124) | copy-start | bytes 3145732
  304.2 6.5 %copy-start.12 = (bf16[8,1,256,256]{3,2,1,0:T(8,128)(2,1)S(1)}, bf16[8,1,256,256]{3,2,1,0:T(8,128)(2,1)}, u32[]{:S(2)}) copy-start(bf16[8,1,256,256]{3,2,1,0:T(8,128)(2,1)} %get-tuple-element.125) | copy-start | bytes 3145732
  310.6 4.2 copy-start.5
Sparse Core Ops, SparseCore 0:
  23.8 170.8 all-gather.2
  322.5 94.9 reduce-scatter.3
where the time goes:
time: 427 us; the launch traced here: 426 us
  waiting for transfers between devices  229 us (54%)
  local copies, waits for them, and re-layouts  72.1 us (17%)
  other arithmetic  52 us (12%)
  matrix products  30 us (7%)
  blocking collectives  23.9 us (6%)
  between operations  18.3 us (4%)
    all_gather x1, waiting for transfers between devices, per_device(): lax.all_gather(owned, 'tile', axis=2, tiled=True)  139 us
    unnamed x3, waiting for transfers between devices  90.5 us
    unnamed x39, local copies, waits for them, and re-layouts  38.4 us
    all_gather x1, blocking collectives, per_device(): lax.all_gather(brightness, 'tile', axis=1, tiled=True)  23.9 us
    dot_general x2, matrix products, predict(): jnp.einsum('tdckr,tckq->tdrq', stacked, cols_f, preferred_element_type=jn...  17.2 us
    dot_general x2, matrix products, pull_back(): jnp.einsum('tdcrq,tckq->tdkr', rstack, cols_f, preferred_element_type=jnp...  12.9 us
    dynamic_slice x1, local copies, waits for them, and re-layouts, per_device(): block_one = lax.dynamic_slice_in_dim(gathered, start_one, span, 3)  12.4 us
    cond x2, local copies, waits for them, and re-layouts, unit_work(): lax.cond(diag_tile, lambda: predict(block_two, block_two, bright_all), la...  10.8 us
  transfers between devices with their start and end apart: 2, of which 2 were waited for; matrix products, arithmetic and copies ran while one was open for 2% of the time, Pallas kernels for 0%

commit v1 on v0

--- a/solution.py
+++ b/solution.py
@@ -7,6 +7,24 @@
 
 BLOCKS = 8
 two_pi = 2.0 * math.pi
+
+
+def gather_around(value, axis, dim):
+    ways, here, hop = (lax.axis_size(axis), lax.axis_index(axis), value.shape[dim])
+    dims = [n * ways if d == dim else n for d, n in enumerate(value.shape)]
+    full = lax.dynamic_update_slice_in_dim(
+        jnp.zeros(dims, value.dtype), value, here * hop, axis=dim
+    )
+    going_up = going_down = value
+    for far in range(1, ways // 2 + 1):
+        going_up = lax.ppermute(going_up, axis, [(d, (d + 1) % ways) for d in range(ways)])
+        full = lax.dynamic_update_slice_in_dim(full, going_up, (here - far) % ways * hop, axis=dim)
+        if 2 * far < ways:
+            going_down = lax.ppermute(going_down, axis, [(d, (d - 1) % ways) for d in range(ways)])
+            full = lax.dynamic_update_slice_in_dim(
+                full, going_down, (here + far) % ways * hop, axis=dim
+            )
+    return full
 
 
 def unit_table(block_count):
@@ -129,7 +147,7 @@
         station_beam, antenna_uvw, source_dirs, source_flux, visible_list
     )
     gathered, bright_all = (
-        lax.all_gather(owned, "tile", axis=2, tiled=True),
+        gather_around(owned, "tile", 2),
         lax.all_gather(brightness, "tile", axis=1, tiled=True),
     )
     residuals = []

time: 427 us -> 2150 us (5.04); the launches traced: 426 us -> 2110 us
  local copies, waits for them, and re-layouts: 72.1 us -> 1560 us
  starting transfers between devices: 0.08 us -> 280 us
  waiting for transfers between devices: 229 us -> 141 us
    dynamic_update_slice x0 -> x16, local copies, waits for them, and re-layouts: none -> 1410 us  [the longest x8 701 us: gather_around(): lax.dynamic_update_slice_in_dim(full, going_up, (here - far) % ways * hop...]
    ppermute x0 -> x15, starting transfers between devices: none -> 279 us  [the longest x8 274 us: gather_around(): lax.ppermute(going_up, axis, [(d, (d + 1) % ways) for d in range(ways)])]
    all_gather x1 -> x0, waiting for transfers between devices: 139 us -> none  [per_device(): lax.all_gather(owned, 'tile', axis=2, tiled=True)]
    ppermute x0 -> x15, local copies, waits for them, and re-layouts: none -> 95.8 us  [the longest x8 50.8 us: gather_around(): lax.ppermute(going_up, axis, [(d, (d + 1) % ways) for d in range(ways)])]
    ppermute x0 -> x15, waiting for transfers between devices: none -> 50.5 us  [the longest x8 50.5 us: gather_around(): lax.ppermute(going_up, axis, [(d, (d + 1) % ways) for d in range(ways)])]
    unnamed x39 -> x83, local copies, waits for them, and re-layouts: 38.4 us -> 10.3 us
    unnamed x3 -> x2, waiting for transfers between devices: 90.5 us -> 90.8 us
  transfers between devices with their start and end apart: 2 -> 16, of which waited for: 2 -> 8; matrix products, arithmetic and copies ran while one was open for 2% -> 68% of each run, Pallas kernels for 0% -> 0%
where the time goes in v1:
time: 2150 us; the launch traced here: 2110 us
  local copies, waits for them, and re-layouts  1560 us (73%)
  starting transfers between devices  280 us (13%)
  waiting for transfers between devices  141 us (7%)
  other arithmetic  53.1 us (2%)
  matrix products  33.3 us (2%)
  blocking collectives  26.6 us (1%)
    dynamic_update_slice x8, local copies, waits for them, and re-layouts, gather_around(): lax.dynamic_update_slice_in_dim(full, going_up, (here - far) % ways * hop...  701 us
    dynamic_update_slice x7, local copies, waits for them, and re-layouts, gather_around(): lax.dynamic_update_slice_in_dim(full, going_down, (here + far) % ways * h...  629 us
    ppermute x8, starting transfers between devices, gather_around(): lax.ppermute(going_up, axis, [(d, (d + 1) % ways) for d in range(ways)])  274 us
    unnamed x2, waiting for transfers between devices  90.8 us
    dynamic_update_slice x1, local copies, waits for them, and re-layouts, gather_around(): lax.dynamic_update_slice_in_dim(jnp.zeros(dims, value.dtype), value, here...  78.6 us
    ppermute x8, local copies, waits for them, and re-layouts, gather_around(): lax.ppermute(going_up, axis, [(d, (d + 1) % ways) for d in range(ways)])  50.8 us
    ppermute x8, waiting for transfers between devices, gather_around(): lax.ppermute(going_up, axis, [(d, (d + 1) % ways) for d in range(ways)])  50.5 us
    ppermute x7, local copies, waits for them, and re-layouts, gather_around(): lax.ppermute(going_down, axis, [(d, (d - 1) % ways) for d in range(ways)])  45 us
  transfers between devices with their start and end apart: 16, of which 8 were waited for; matrix products, arithmetic and copies ran while one was open for 68% of the time, Pallas kernels for 0%

profile of v1, /device:TPU:0, one launch (start us, length us, event | category | flops | bytes accessed | tf_op | source)
XLA Modules:
  0.0 2111.4 jit_solution(16064458773416065701)
XLA Ops:
  12.0 8.9 add_convert_fusion
  26.7 23.8 %collective-permute-done = bf16[8,2,32,2048]{3,2,1,0:T(8,128)(2,1)S(1)} collective-permute-done((bf16[8,2,32,2048]{3,2,1,0:T(8,128)(2,1)S(1)}, bf16[8,2,32,2048]{3,2,1,0:T(8,128)(2,1)S(1)}, u32[]{:S(2)}, u32[]{:S(2)}) %collective-permute-start) | collective-permute-done | bytes 2097184 | tf_op jit(solution)/shard_map/ppermute | solution.py:20
  50.5 19.3 collective-permute-start.2
  71.1 7.6 collective-permute-done.2
  78.8 38.9 %collective-permute-start.4 = (bf16[8,2,32,2048]{3,2,1,0:T(8,128)(2,1)S(1)}, bf16[8,2,32,2048]{3,2,1,0:T(8,128)(2,1)S(1)}, u32[]{:S(2)}, u32[]{:S(2)}) collective-permute-start(bf16[8,2,32,2048]{3,2,1,0:T(8,128)(2,1)S(1)} %collective-permute-done.2), channel_id=1, source_target_pairs={{0,1},{1,2},{2,3},{3,4},{4,5},{5,6},{6,7},{7,8},{8,9},{9,10},{10,1... | collective-permute-start | bytes 6291464 | tf_op jit(solution)/shard_map/ppermute | solution.py:20
  121.9 43.0 %collective-permute-start.6 = (bf16[8,2,32,2048]{3,2,1,0:T(8,128)(2,1)S(1)}, bf16[8,2,32,2048]{3,2,1,0:T(8,128)(2,1)S(1)}, u32[]{:S(2)}, u32[]{:S(2)}) collective-permute-start(bf16[8,2,32,2048]{3,2,1,0:T(8,128)(2,1)S(1)} %collective-permute-done.4), channel_id=1, source_target_pairs={{0,1},{1,2},{2,3},{3,4},{4,5},{5,6},{6,7},{7,8},{8,9},{9,10},{10,1... | collective-permute-start | bytes 6291464 | tf_op jit(solution)/shard_map/ppermute | solution.py:20
  168.7 43.4 %collective-permute-start.8 = (bf16[8,2,32,2048]{3,2,1,0:T(8,128)(2,1)S(1)}, bf16[8,2,32,2048]{3,2,1,0:T(8,128)(2,1)S(1)}, u32[]{:S(2)}, u32[]{:S(2)}) collective-permute-start(bf16[8,2,32,2048]{3,2,1,0:T(8,128)(2,1)S(1)} %collective-permute-done.6), channel_id=1, source_target_pairs={{0,1},{1,2},{2,3},{3,4},{4,5},{5,6},{6,7},{7,8},{8,9},{9,10},{10,1... | collective-permute-start | bytes 6291464 | tf_op jit(solution)/shard_map/ppermute | solution.py:20
  215.9 42.7 %collective-permute-start.10 = (bf16[8,2,32,2048]{3,2,1,0:T(8,128)(2,1)S(1)}, bf16[8,2,32,2048]{3,2,1,0:T(8,128)(2,1)S(1)}, u32[]{:S(2)}, u32[]{:S(2)}) collective-permute-start(bf16[8,2,32,2048]{3,2,1,0:T(8,128)(2,1)S(1)} %collective-permute-done.8), channel_id=1, source_target_pairs={{0,1},{1,2},{2,3},{3,4},{4,5},{5,6},{6,7},{7,8},{8,9},{9,10},{10,1... | collective-permute-start | bytes 6291464 | tf_op jit(solution)/shard_map/ppermute | solution.py:20
  262.4 42.8 %collective-permute-start.12 = (bf16[8,2,32,2048]{3,2,1,0:T(8,128)(2,1)S(1)}, bf16[8,2,32,2048]{3,2,1,0:T(8,128)(2,1)}, u32[]{:S(2)}, u32[]{:S(2)}) collective-permute-start(bf16[8,2,32,2048]{3,2,1,0:T(8,128)(2,1)S(1)} %collective-permute-done.10), channel_id=1, source_target_pairs={{0,1},{1,2},{2,3},{3,4},{4,5},{5,6},{6,7},{7,8},{8,9},{9,10},{10,1... | collective-permute-start | bytes 6291464 | tf_op jit(solution)/shard_map/ppermute | solution.py:20
  309.2 43.5 %collective-permute-start.14 = (bf16[8,2,32,2048]{3,2,1,0:T(8,128)(2,1)}, bf16[8,2,32,2048]{3,2,1,0:T(8,128)(2,1)}, u32[]{:S(2)}, u32[]{:S(2)}) collective-permute-start(bf16[8,2,32,2048]{3,2,1,0:T(8,128)(2,1)} %collective-permute-done.12), channel_id=1, source_target_pairs={{0,1},{1,2},{2,3},{3,4},{4,5},{5,6},{6,7},{7,8},{8,9},{9,10},{10,1... | collective-permute-start | bytes 6291464 | tf_op jit(solution)/shard_map/ppermute | solution.py:20
  363.6 26.6 %all-gather = bf16[16,32,8]{1,2,0:T(8,128)(2,1)S(1)} all-gather(bf16[1,32,8]{1,2,0:T(8,128)(2,1)S(1)} %bitcast.185), channel_id=1, replica_groups=mesh['grp'=2,'tile'=16] {'tile'}, dimensions={0}, use_global_device_ids=true | all-gather | bytes 8704 | tf_op jit(solution)/shard_map/all_gather | solution.py:151
  390.6 10.9 broadcast_in_dim.106
  401.5 78.6 %dynamic_update_slice.48 = bf16[8,2,512,2048]{2,3,1,0:T(8,128)(2,1)} dynamic-update-slice(bf16[8,2,512,2048]{2,3,1,0:T(8,128)(2,1)} %broadcast_in_dim.106, bf16[8,2,32,2048]{2,3,1,0:T(8,128)(2,1)} %copy.126, s32[]{:T(128)} %constant.129.clone.1, s32[]{:T(128)} %constant.129.clone.1, s32[]{:T(128)S(6)} %select_n.210, s32[]{:T(128)} %constant.129.clone.1) | dynamic-update-slice | bytes 4194308 | tf_op jit(solution)/shard_map/dynamic_update_slice | solution.py:15
  484.2 5.9 copy.127
  490.1 90.2 %dynamic_update_slice.49 = bf16[8,2,512,2048]{2,3,1,0:T(8,128)(2,1)} dynamic-update-slice(bf16[8,2,512,2048]{2,3,1,0:T(8,128)(2,1)} %dynamic_update_slice.48, bf16[8,2,32,2048]{2,3,1,0:T(8,128)(2,1)} %copy.127, s32[]{:T(128)} %constant.129.clone.1, s32[]{:T(128)} %constant.129.clone.1, s32[]{:T(128)S(6)} %select_n.212, s32[]{:T(128)} %constant.129.clone.1) | dynamic-update-slice | bytes 4194308 | tf_op jit(solution)/shard_map/dynamic_update_slice | solution.py:21
  580.3 5.9 copy.128
  586.2 91.8 %dynamic_update_slice.50 = bf16[8,2,512,2048]{2,3,1,0:T(8,128)(2,1)} dynamic-update-slice(bf16[8,2,512,2048]{2,3,1,0:T(8,128)(2,1)} %dynamic_update_slice.49, bf16[8,2,32,2048]{2,3,1,0:T(8,128)(2,1)} %copy.128, s32[]{:T(128)} %constant.129.clone.1, s32[]{:T(128)} %constant.129.clone.1, s32[]{:T(128)S(6)} %select_n.214, s32[]{:T(128)} %constant.129.clone.1) | dynamic-update-slice | bytes 4194308 | tf_op jit(solution)/shard_map/dynamic_update_slice | solution.py:24
  678.0 5.9 copy.129
  683.9 90.2 %dynamic_update_slice.51 = bf16[8,2,512,2048]{2,3,1,0:T(8,128)(2,1)} dynamic-update-slice(bf16[8,2,512,2048]{2,3,1,0:T(8,128)(2,1)} %dynamic_update_slice.50, bf16[8,2,32,2048]{2,3,1,0:T(8,128)(2,1)} %copy.129, s32[]{:T(128)} %constant.129.clone.1, s32[]{:T(128)} %constant.129.clone.1, s32[]{:T(128)S(6)} %select_n.216, s32[]{:T(128)} %constant.129.clone.1) | dynamic-update-slice | bytes 4194308 | tf_op jit(solution)/shard_map/dynamic_update_slice | solution.py:21
  774.1 5.9 copy.130
  780.0 91.8 %dynamic_update_slice.52 = bf16[8,2,512,2048]{2,3,1,0:T(8,128)(2,1)} dynamic-update-slice(bf16[8,2,512,2048]{2,3,1,0:T(8,128)(2,1)} %dynamic_update_slice.51, bf16[8,2,32,2048]{2,3,1,0:T(8,128)(2,1)} %copy.130, s32[]{:T(128)} %constant.129.clone.1, s32[]{:T(128)} %constant.129.clone.1, s32[]{:T(128)S(6)} %select_n.218, s32[]{:T(128)} %constant.129.clone.1) | dynamic-update-slice | bytes 4194308 | tf_op jit(solution)/shard_map/dynamic_update_slice | solution.py:24
  871.8 5.9 copy.131
  877.7 90.2 %dynamic_update_slice.53 = bf16[8,2,512,2048]{2,3,1,0:T(8,128)(2,1)} dynamic-update-slice(bf16[8,2,512,2048]{2,3,1,0:T(8,128)(2,1)} %dynamic_update_slice.52, bf16[8,2,32,2048]{2,3,1,0:T(8,128)(2,1)} %copy.131, s32[]{:T(128)} %constant.129.clone.1, s32[]{:T(128)} %constant.129.clone.1, s32[]{:T(128)S(6)} %select_n.220, s32[]{:T(128)} %constant.129.clone.1) | dynamic-update-slice | bytes 4194308 | tf_op jit(solution)/shard_map/dynamic_update_slice | solution.py:21
  967.9 5.9 copy.132
  973.8 91.8 %dynamic_update_slice.54 = bf16[8,2,512,2048]{2,3,1,0:T(8,128)(2,1)} dynamic-update-slice(bf16[8,2,512,2048]{2,3,1,0:T(8,128)(2,1)} %dynamic_update_slice.53, bf16[8,2,32,2048]{2,3,1,0:T(8,128)(2,1)} %copy.132, s32[]{:T(128)} %constant.129.clone.1, s32[]{:T(128)} %constant.129.clone.1, s32[]{:T(128)S(6)} %select_n.222, s32[]{:T(128)} %constant.129.clone.1) | dynamic-update-slice | bytes 4194308 | tf_op jit(solution)/shard_map/dynamic_update_slice | solution.py:24
  1071.5 76.7 %dynamic_update_slice.55 = bf16[8,2,512,2048]{2,3,1,0:T(8,128)(2,1)} dynamic-update-slice(bf16[8,2,512,2048]{2,3,1,0:T(8,128)(2,1)} %dynamic_update_slice.54, bf16[8,2,32,2048]{2,3,1,0:T(8,128)(2,1)} %copy.133, s32[]{:T(128)} %constant.129.clone.1, s32[]{:T(128)} %constant.129.clone.1, s32[]{:T(128)S(6)} %select_n.224, s32[]{:T(128)} %constant.129.clone.1) | dynamic-update-slice | bytes 4194308 | tf_op jit(solution)/shard_map/dynamic_update_slice | solution.py:21
  1148.3 5.9 copy.134
  1154.2 78.6 %dynamic_update_slice.56 = bf16[8,2,512,2048]{2,3,1,0:T(8,128)(2,1)} dynamic-update-slice(bf16[8,2,512,2048]{2,3,1,0:T(8,128)(2,1)} %dynamic_update_slice.55, bf16[8,2,32,2048]{2,3,1,0:T(8,128)(2,1)} %copy.134, s32[]{:T(128)} %constant.129.clone.1, s32[]{:T(128)} %constant.129.clone.1, s32[]{:T(128)S(6)} %select_n.226, s32[]{:T(128)} %constant.129.clone.1) | dynamic-update-slice | bytes 4194308 | tf_op jit(solution)/shard_map/dynamic_update_slice | solution.py:24
  1238.7 91.8 %dynamic_update_slice.57 = bf16[8,2,512,2048]{2,3,1,0:T(8,128)(2,1)} dynamic-update-slice(bf16[8,2,512,2048]{2,3,1,0:T(8,128)(2,1)} %dynamic_update_slice.56, bf16[8,2,32,2048]{2,3,1,0:T(8,128)(2,1)} %copy.135, s32[]{:T(128)} %constant.129.clone.1, s32[]{:T(128)} %constant.129.clone.1, s32[]{:T(128)S(6)} %select_n.228, s32[]{:T(128)} %constant.129.clone.1) | dynamic-update-slice | bytes 4194308 | tf_op jit(solution)/shard_map/dynamic_update_slice | solution.py:21
  1330.5 5.9 copy.136
  1336.4 91.8 %dynamic_update_slice.58 = bf16[8,2,512,2048]{2,3,1,0:T(8,128)(2,1)} dynamic-update-slice(bf16[8,2,512,2048]{2,3,1,0:T(8,128)(2,1)} %dynamic_update_slice.57, bf16[8,2,32,2048]{2,3,1,0:T(8,128)(2,1)} %copy.136, s32[]{:T(128)} %constant.129.clone.1, s32[]{:T(128)} %constant.129.clone.1, s32[]{:T(128)S(6)} %select_n.230, s32[]{:T(128)} %constant.129.clone.1) | dynamic-update-slice | bytes 4194308 | tf_op jit(solution)/shard_map/dynamic_update_slice | solution.py:24
  1428.2 5.9 copy.137
  1434.1 91.7 %dynamic_update_slice.59 = bf16[8,2,512,2048]{2,3,1,0:T(8,128)(2,1)} dynamic-update-slice(bf16[8,2,512,2048]{2,3,1,0:T(8,128)(2,1)} %dynamic_update_slice.58, bf16[8,2,32,2048]{2,3,1,0:T(8,128)(2,1)} %copy.137, s32[]{:T(128)} %constant.129.clone.1, s32[]{:T(128)} %constant.129.clone.1, s32[]{:T(128)S(6)} %select_n.232, s32[]{:T(128)} %constant.129.clone.1) | dynamic-update-slice | bytes 4194308 | tf_op jit(solution)/shard_map/dynamic_update_slice | solution.py:21
  1525.8 7.8 copy.138
  1533.6 91.7 %dynamic_update_slice.60 = bf16[8,2,512,2048]{2,3,1,0:T(8,128)(2,1)} dynamic-update-slice(bf16[8,2,512,2048]{2,3,1,0:T(8,128)(2,1)} %dynamic_update_slice.59, bf16[8,2,32,2048]{2,3,1,0:T(8,128)(2,1)} %copy.138, s32[]{:T(128)} %constant.129.clone.1, s32[]{:T(128)} %constant.129.clone.1, s32[]{:T(128)S(6)} %select_n.234, s32[]{:T(128)} %constant.129.clone.1) | dynamic-update-slice | bytes 4194308 | tf_op jit(solution)/shard_map/dynamic_update_slice | solution.py:24
  1625.3 7.8 copy.139
  1633.0 91.7 %dynamic_update_slice.61 = bf16[8,2,512,2048]{2,3,1,0:T(8,128)(2,1)} dynamic-update-slice(bf16[8,2,512,2048]{2,3,1,0:T(8,128)(2,1)} %dynamic_update_slice.60, bf16[8,2,32,2048]{2,3,1,0:T(8,128)(2,1)} %copy.139, s32[]{:T(128)} %constant.129.clone.1, s32[]{:T(128)} %constant.129.clone.1, s32[]{:T(128)S(6)} %select_n.236, s32[]{:T(128)} %constant.129.clone.1) | dynamic-update-slice | bytes 4194308 | tf_op jit(solution)/shard_map/dynamic_update_slice | solution.py:21
  1724.7 7.8 copy.140
  1732.5 91.7 %dynamic_update_slice.62 = bf16[8,2,512,2048]{2,3,1,0:T(8,128)(2,1)} dynamic-update-slice(bf16[8,2,512,2048]{2,3,1,0:T(8,128)(2,1)} %dynamic_update_slice.61, bf16[8,2,32,2048]{2,3,1,0:T(8,128)(2,1)} %copy.140, s32[]{:T(128)} %constant.129.clone.1, s32[]{:T(128)} %constant.129.clone.1, s32[]{:T(128)S(6)} %select_n.238, s32[]{:T(128)} %constant.129.clone.1) | dynamic-update-slice | bytes 4194308 | tf_op jit(solution)/shard_map/dynamic_update_slice | solution.py:24
  1824.2 7.8 copy.141
  1831.9 78.7 %dynamic_update_slice.63 = bf16[8,2,512,2048]{2,3,1,0:T(8,128)(2,1)} dynamic-update-slice(bf16[8,2,512,2048]{2,3,1,0:T(8,128)(2,1)} %dynamic_update_slice.62, bf16[8,2,32,2048]{2,3,1,0:T(8,128)(2,1)} %copy.141, s32[]{:T(128)} %constant.129.clone.1, s32[]{:T(128)} %constant.129.clone.1, s32[]{:T(128)S(6)} %select_n.240, s32[]{:T(128)} %constant.129.clone.1) | dynamic-update-slice | bytes 4194308 | tf_op jit(solution)/shard_map/dynamic_update_slice | solution.py:21
  1910.6 7.8 constant_dynamic-slice_fusion.3
  1918.4 7.5 fusion.44
  1942.1 9.1 broadcast_select_fusion.3
  1969.7 9.0 broadcast_select_fusion.2
  1986.2 7.5 fusion.45
  1999.5 7.7 fusion.47
  2012.1 90.8 %reduce-scatter.4.cloned.1.call-done = f32[32,8]{1,0:T(8,128)} async-done(((f32[512,8]{1,0:T(8,128)}), f32[32,8]{1,0:T(8,128)}) %reduce-scatter.4.cloned.1.call-update) | async-done | bytes 1040
  (150 shorter events, 113.7 us)
Async XLA Ops:
  7.2 4.5 copy-start.42
  7.2 2095.7 %reduce-scatter.4.cloned.1.call-start = ((), (), s32[]{:S(2)}) async-start(), calls=%async_computation.1 | async-start | bytes 278528
  21.1 29.3 %collective-permute-start = (bf16[8,2,32,2048]{3,2,1,0:T(8,128)(2,1)S(1)}, bf16[8,2,32,2048]{3,2,1,0:T(8,128)(2,1)S(1)}, u32[]{:S(2)}, u32[]{:S(2)}) collective-permute-start(bf16[8,2,32,2048]{3,2,1,0:T(8,128)(2,1)S(1)} %pad_maximum_fusion.4), channel_id=1, source_target_pairs={{0,1},{1,2},{2,3},{3,4},{4,5},{5,6},{6,7},{7,8},{8,9},{9,10},{10,1... | collective-permute-start | bytes 6291464 | tf_op jit(solution)/shard_map/ppermute | solution.py:20
  21.7 48.1 %collective-permute-start.1 = (bf16[8,2,32,2048]{3,2,1,0:T(8,128)(2,1)S(1)}, bf16[8,2,32,2048]{3,2,1,0:T(8,128)(2,1)S(1)}, u32[]{:S(2)}, u32[]{:S(2)}) collective-permute-start(bf16[8,2,32,2048]{3,2,1,0:T(8,128)(2,1)S(1)} %pad_maximum_fusion.4), channel_id=1, source_target_pairs={{0,15},{1,0},{2,1},{3,2},{4,3},{5,4},{6,5},{7,6},{8,7},{9,8},{10,9... | collective-permute-start | bytes 6291464 | tf_op jit(solution)/shard_map/ppermute | solution.py:23
  50.5 71.4 %copy-start.21 = (bf16[8,2,32,2048]{3,2,1,0:T(8,128)(2,1)}, bf16[8,2,32,2048]{3,2,1,0:T(8,128)(2,1)S(1)}, u32[]{:S(2)}) copy-start(bf16[8,2,32,2048]{3,2,1,0:T(8,128)(2,1)S(1)} %collective-permute-done) | copy-start | bytes 6291460
  50.5 28.3 %collective-permute-start.2 = (bf16[8,2,32,2048]{3,2,1,0:T(8,128)(2,1)S(1)}, bf16[8,2,32,2048]{3,2,1,0:T(8,128)(2,1)S(1)}, u32[]{:S(2)}, u32[]{:S(2)}) collective-permute-start(bf16[8,2,32,2048]{3,2,1,0:T(8,128)(2,1)S(1)} %collective-permute-done), channel_id=1, source_target_pairs={{0,1},{1,2},{2,3},{3,4},{4,5},{5,6},{6,7},{7,8},{8,9},{9,10},{10,1... | collective-permute-start | bytes 6291464 | tf_op jit(solution)/shard_map/ppermute | solution.py:20
  71.1 46.6 %collective-permute-start.3 = (bf16[8,2,32,2048]{3,2,1,0:T(8,128)(2,1)S(1)}, bf16[8,2,32,2048]{3,2,1,0:T(8,128)(2,1)S(1)}, u32[]{:S(2)}, u32[]{:S(2)}) collective-permute-start(bf16[8,2,32,2048]{3,2,1,0:T(8,128)(2,1)S(1)} %collective-permute-done.1), channel_id=1, source_target_pairs={{0,15},{1,0},{2,1},{3,2},{4,3},{5,4},{6,5},{7,6},{8,7},{9,8},{10,9... | collective-permute-start | bytes 6291464 | tf_op jit(solution)/shard_map/ppermute | solution.py:23
  78.7 38.9 %copy-start.19 = (bf16[8,2,32,2048]{3,2,1,0:T(8,128)(2,1)}, bf16[8,2,32,2048]{3,2,1,0:T(8,128)(2,1)S(1)}, u32[]{:S(2)}) copy-start(bf16[8,2,32,2048]{3,2,1,0:T(8,128)(2,1)S(1)} %collective-permute-done.2) | copy-start | bytes 6291460
  78.8 43.1 %collective-permute-start.4 = (bf16[8,2,32,2048]{3,2,1,0:T(8,128)(2,1)S(1)}, bf16[8,2,32,2048]{3,2,1,0:T(8,128)(2,1)S(1)}, u32[]{:S(2)}, u32[]{:S(2)}) collective-permute-start(bf16[8,2,32,2048]{3,2,1,0:T(8,128)(2,1)S(1)} %collective-permute-done.2), channel_id=1, source_target_pairs={{0,1},{1,2},{2,3},{3,4},{4,5},{5,6},{6,7},{7,8},{8,9},{9,10},{10,1... | collective-permute-start | bytes 6291464 | tf_op jit(solution)/shard_map/ppermute | solution.py:20
  117.7 47.2 %copy-start.23 = (bf16[8,2,32,2048]{3,2,1,0:T(8,128)(2,1)}, bf16[8,2,32,2048]{3,2,1,0:T(8,128)(2,1)S(1)}, u32[]{:S(2)}) copy-start(bf16[8,2,32,2048]{3,2,1,0:T(8,128)(2,1)S(1)} %collective-permute-done.3) | copy-start | bytes 6291460
  117.7 47.2 %collective-permute-start.5 = (bf16[8,2,32,2048]{3,2,1,0:T(8,128)(2,1)S(1)}, bf16[8,2,32,2048]{3,2,1,0:T(8,128)(2,1)S(1)}, u32[]{:S(2)}, u32[]{:S(2)}) collective-permute-start(bf16[8,2,32,2048]{3,2,1,0:T(8,128)(2,1)S(1)} %collective-permute-done.3), channel_id=1, source_target_pairs={{0,15},{1,0},{2,1},{3,2},{4,3},{5,4},{6,5},{7,6},{8,7},{9,8},{10,9... | collective-permute-start | bytes 6291464 | tf_op jit(solution)/shard_map/ppermute | solution.py:23
  121.9 43.0 %copy-start.25 = (bf16[8,2,32,2048]{3,2,1,0:T(8,128)(2,1)}, bf16[8,2,32,2048]{3,2,1,0:T(8,128)(2,1)S(1)}, u32[]{:S(2)}) copy-start(bf16[8,2,32,2048]{3,2,1,0:T(8,128)(2,1)S(1)} %collective-permute-done.4) | copy-start | bytes 6291460
  121.9 46.8 %collective-permute-start.6 = (bf16[8,2,32,2048]{3,2,1,0:T(8,128)(2,1)S(1)}, bf16[8,2,32,2048]{3,2,1,0:T(8,128)(2,1)S(1)}, u32[]{:S(2)}, u32[]{:S(2)}) collective-permute-start(bf16[8,2,32,2048]{3,2,1,0:T(8,128)(2,1)S(1)} %collective-permute-done.4), channel_id=1, source_target_pairs={{0,1},{1,2},{2,3},{3,4},{4,5},{5,6},{6,7},{7,8},{8,9},{9,10},{10,1... | collective-permute-start | bytes 6291464 | tf_op jit(solution)/shard_map/ppermute | solution.py:20
  164.9 47.2 %collective-permute-start.7 = (bf16[8,2,32,2048]{3,2,1,0:T(8,128)(2,1)S(1)}, bf16[8,2,32,2048]{3,2,1,0:T(8,128)(2,1)S(1)}, u32[]{:S(2)}, u32[]{:S(2)}) collective-permute-start(bf16[8,2,32,2048]{3,2,1,0:T(8,128)(2,1)S(1)} %collective-permute-done.5), channel_id=1, source_target_pairs={{0,15},{1,0},{2,1},{3,2},{4,3},{5,4},{6,5},{7,6},{8,7},{9,8},{10,9... | collective-permute-start | bytes 6291464 | tf_op jit(solution)/shard_map/ppermute | solution.py:23
  168.7 43.5 %copy-start.29 = (bf16[8,2,32,2048]{3,2,1,0:T(8,128)(2,1)}, bf16[8,2,32,2048]{3,2,1,0:T(8,128)(2,1)S(1)}, u32[]{:S(2)}) copy-start(bf16[8,2,32,2048]{3,2,1,0:T(8,128)(2,1)S(1)} %collective-permute-done.6) | copy-start | bytes 6291460
  168.7 47.2 %collective-permute-start.8 = (bf16[8,2,32,2048]{3,2,1,0:T(8,128)(2,1)S(1)}, bf16[8,2,32,2048]{3,2,1,0:T(8,128)(2,1)S(1)}, u32[]{:S(2)}, u32[]{:S(2)}) collective-permute-start(bf16[8,2,32,2048]{3,2,1,0:T(8,128)(2,1)S(1)} %collective-permute-done.6), channel_id=1, source_target_pairs={{0,1},{1,2},{2,3},{3,4},{4,5},{5,6},{6,7},{7,8},{8,9},{9,10},{10,1... | collective-permute-start | bytes 6291464 | tf_op jit(solution)/shard_map/ppermute | solution.py:20
  212.2 46.5 %collective-permute-start.9 = (bf16[8,2,32,2048]{3,2,1,0:T(8,128)(2,1)S(1)}, bf16[8,2,32,2048]{3,2,1,0:T(8,128)(2,1)S(1)}, u32[]{:S(2)}, u32[]{:S(2)}) collective-permute-start(bf16[8,2,32,2048]{3,2,1,0:T(8,128)(2,1)S(1)} %collective-permute-done.7), channel_id=1, source_target_pairs={{0,15},{1,0},{2,1},{3,2},{4,3},{5,4},{6,5},{7,6},{8,7},{9,8},{10,9... | collective-permute-start | bytes 6291464 | tf_op jit(solution)/shard_map/ppermute | solution.py:23
  215.9 42.7 %copy-start.33 = (bf16[8,2,32,2048]{3,2,1,0:T(8,128)(2,1)}, bf16[8,2,32,2048]{3,2,1,0:T(8,128)(2,1)S(1)}, u32[]{:S(2)}) copy-start(bf16[8,2,32,2048]{3,2,1,0:T(8,128)(2,1)S(1)} %collective-permute-done.8) | copy-start | bytes 6291460
  215.9 46.5 %collective-permute-start.10 = (bf16[8,2,32,2048]{3,2,1,0:T(8,128)(2,1)S(1)}, bf16[8,2,32,2048]{3,2,1,0:T(8,128)(2,1)S(1)}, u32[]{:S(2)}, u32[]{:S(2)}) collective-permute-start(bf16[8,2,32,2048]{3,2,1,0:T(8,128)(2,1)S(1)} %collective-permute-done.8), channel_id=1, source_target_pairs={{0,1},{1,2},{2,3},{3,4},{4,5},{5,6},{6,7},{7,8},{8,9},{9,10},{10,1... | collective-permute-start | bytes 6291464 | tf_op jit(solution)/shard_map/ppermute | solution.py:20
  258.6 46.6 %collective-permute-start.11 = (bf16[8,2,32,2048]{3,2,1,0:T(8,128)(2,1)S(1)}, bf16[8,2,32,2048]{3,2,1,0:T(8,128)(2,1)}, u32[]{:S(2)}, u32[]{:S(2)}) collective-permute-start(bf16[8,2,32,2048]{3,2,1,0:T(8,128)(2,1)S(1)} %collective-permute-done.9), channel_id=1, source_target_pairs={{0,15},{1,0},{2,1},{3,2},{4,3},{5,4},{6,5},{7,6},{8,7},{9,8},{10,9... | collective-permute-start | bytes 6291464 | tf_op jit(solution)/shard_map/ppermute | solution.py:23
  262.4 42.8 %copy-start.37 = (bf16[8,2,32,2048]{3,2,1,0:T(8,128)(2,1)}, bf16[8,2,32,2048]{3,2,1,0:T(8,128)(2,1)S(1)}, u32[]{:S(2)}) copy-start(bf16[8,2,32,2048]{3,2,1,0:T(8,128)(2,1)S(1)} %collective-permute-done.10) | copy-start | bytes 6291460
  262.4 46.7 %collective-permute-start.12 = (bf16[8,2,32,2048]{3,2,1,0:T(8,128)(2,1)S(1)}, bf16[8,2,32,2048]{3,2,1,0:T(8,128)(2,1)}, u32[]{:S(2)}, u32[]{:S(2)}) collective-permute-start(bf16[8,2,32,2048]{3,2,1,0:T(8,128)(2,1)S(1)} %collective-permute-done.10), channel_id=1, source_target_pairs={{0,1},{1,2},{2,3},{3,4},{4,5},{5,6},{6,7},{7,8},{8,9},{9,10},{10,1... | collective-permute-start | bytes 6291464 | tf_op jit(solution)/shard_map/ppermute | solution.py:20
  305.2 1419.5 %collective-permute-start.13 = (bf16[8,2,32,2048]{3,2,1,0:T(8,128)(2,1)}, bf16[8,2,32,2048]{3,2,1,0:T(8,128)(2,1)}, u32[]{:S(2)}, u32[]{:S(2)}) collective-permute-start(bf16[8,2,32,2048]{3,2,1,0:T(8,128)(2,1)} %collective-permute-done.11), channel_id=1, source_target_pairs={{0,15},{1,0},{2,1},{3,2},{4,3},{5,4},{6,5},{7,6},{8,7},{9,8},{10,9... | collective-permute-start | bytes 6291464 | tf_op jit(solution)/shard_map/ppermute | solution.py:23
  309.2 1515.0 %collective-permute-start.14 = (bf16[8,2,32,2048]{3,2,1,0:T(8,128)(2,1)}, bf16[8,2,32,2048]{3,2,1,0:T(8,128)(2,1)}, u32[]{:S(2)}, u32[]{:S(2)}) collective-permute-start(bf16[8,2,32,2048]{3,2,1,0:T(8,128)(2,1)} %collective-permute-done.12), channel_id=1, source_target_pairs={{0,1},{1,2},{2,3},{3,4},{4,5},{5,6},{6,7},{7,8},{8,9},{9,10},{10,1... | collective-permute-start | bytes 6291464 | tf_op jit(solution)/shard_map/ppermute | solution.py:20
  352.6 5.9 copy-start.44
  352.6 5.9 copy-start.45
  352.6 9.0 copy-start.43
  401.5 78.6 %copy-start.40 = (s32[8,2048]{1,0:T(8,128)S(1)}, s32[8,2048]{1,0:T(8,128)}, u32[]{:S(2)}) copy-start(s32[8,2048]{1,0:T(8,128)} %param.24) | copy-start | bytes 196612
  480.1 4.1 copy-start.22
  490.1 90.2 %copy-start.18 = (bf16[8,2,32,2048]{3,2,1,0:T(8,128)(2,1)S(1)}, bf16[8,2,32,2048]{3,2,1,0:T(8,128)(2,1)}, u32[]{:S(2)}) copy-start(bf16[8,2,32,2048]{3,2,1,0:T(8,128)(2,1)} %copy-done.17) | copy-start | bytes 6291460
  586.2 91.8 %copy-start.20 = (bf16[8,2,32,2048]{3,2,1,0:T(8,128)(2,1)S(1)}, bf16[8,2,32,2048]{3,2,1,0:T(8,128)(2,1)}, u32[]{:S(2)}) copy-start(bf16[8,2,32,2048]{3,2,1,0:T(8,128)(2,1)} %copy-done.19) | copy-start | bytes 6291460
  683.9 90.2 %copy-start.24 = (bf16[8,2,32,2048]{3,2,1,0:T(8,128)(2,1)S(1)}, bf16[8,2,32,2048]{3,2,1,0:T(8,128)(2,1)}, u32[]{:S(2)}) copy-start(bf16[8,2,32,2048]{3,2,1,0:T(8,128)(2,1)} %copy-done.23) | copy-start | bytes 6291460
  780.0 91.8 %copy-start.26 = (bf16[8,2,32,2048]{3,2,1,0:T(8,128)(2,1)S(1)}, bf16[8,2,32,2048]{3,2,1,0:T(8,128)(2,1)}, u32[]{:S(2)}) copy-start(bf16[8,2,32,2048]{3,2,1,0:T(8,128)(2,1)} %copy-done.25) | copy-start | bytes 6291460
  877.7 90.2 %copy-start.28 = (bf16[8,2,32,2048]{3,2,1,0:T(8,128)(2,1)S(1)}, bf16[8,2,32,2048]{3,2,1,0:T(8,128)(2,1)}, u32[]{:S(2)}) copy-start(bf16[8,2,32,2048]{3,2,1,0:T(8,128)(2,1)} %copy-done.27) | copy-start | bytes 6291460
  973.8 91.8 %copy-start.30 = (bf16[8,2,32,2048]{3,2,1,0:T(8,128)(2,1)S(1)}, bf16[8,2,32,2048]{3,2,1,0:T(8,128)(2,1)}, u32[]{:S(2)}) copy-start(bf16[8,2,32,2048]{3,2,1,0:T(8,128)(2,1)} %copy-done.29) | copy-start | bytes 6291460
  1071.5 76.7 %copy-start.32 = (bf16[8,2,32,2048]{3,2,1,0:T(8,128)(2,1)S(1)}, bf16[8,2,32,2048]{3,2,1,0:T(8,128)(2,1)}, u32[]{:S(2)}) copy-start(bf16[8,2,32,2048]{3,2,1,0:T(8,128)(2,1)} %copy-done.31) | copy-start | bytes 6291460
  1154.1 78.6 %copy-start.34 = (bf16[8,2,32,2048]{3,2,1,0:T(8,128)(2,1)S(1)}, bf16[8,2,32,2048]{3,2,1,0:T(8,128)(2,1)}, u32[]{:S(2)}) copy-start(bf16[8,2,32,2048]{3,2,1,0:T(8,128)(2,1)} %copy-done.33) | copy-start | bytes 6291460
  1238.7 91.9 %copy-start.36 = (bf16[8,2,32,2048]{3,2,1,0:T(8,128)(2,1)S(1)}, bf16[8,2,32,2048]{3,2,1,0:T(8,128)(2,1)}, u32[]{:S(2)}) copy-start(bf16[8,2,32,2048]{3,2,1,0:T(8,128)(2,1)} %copy-done.35) | copy-start | bytes 6291460
  1336.4 91.8 %copy-start.38 = (bf16[8,2,32,2048]{3,2,1,0:T(8,128)(2,1)S(1)}, bf16[8,2,32,2048]{3,2,1,0:T(8,128)(2,1)}, u32[]{:S(2)}) copy-start(bf16[8,2,32,2048]{3,2,1,0:T(8,128)(2,1)} %copy-done.37) | copy-start | bytes 6291460
  1936.5 4.3 copy-start.4
  1936.5 5.6 copy-start.11
  1958.7 9.7 copy-start.41
  1964.0 4.3 copy-start
  1964.0 5.6 copy-start.9
  1969.7 9.0 copy-start.39
  1980.5 5.8 copy-start.5
  1994.0 5.5 copy-start.1
  1999.5 8.5 copy-start.12
  (8 other events, 21.2 us)
Sparse Core Ops, SparseCore 0:
  2008.2 94.6 reduce-scatter.3
